TPU v7x, 32 devices: a whole 2x2x4 slice. The times are simulated.
32 devices in a mesh: tm: 8 (over y, x, core), space: 4 (over z).
Axes of the slice: x: 2, y: 2, z: 4, core: 2. Of those that a mesh axis runs over, the one named last changes fastest.
Arguments:
- increments: float32 [16, 256, 2048], P('tm', 'space'), may hold values from -6 to 6
- precision: float32 [16, 256, 2048], P('tm', 'space'), may hold values from 0.5 to 4
- courant_rows: float32 [256, 2048], P('space'), may hold values from 0.05 to 0.45
- courant_cols: float32 [256, 2048], P('space'), may hold values from 0.05 to 0.45
- wind_codes: int32 [16, 32, 16], P('tm', 'space'), may hold values from 0 to 3
Outputs:
- misfit: float32 [16, 256, 2048], P('tm', 'space')
- adjoint_image: float32 [16, 256, 2048], P('tm', 'space')
All inputs are finite; a program needn't handle non-finite values.
Results may differ from a plain program's by a relative error of at most 0.00002.
Values sent between devices are 32-bit elements; how exact they have to be, the bound alone decides.
A program may use at most 64 MiB of HBM per device.

v0:
```python
import jax
import jax.numpy as jnp
from jax import lax
from jax.sharding import PartitionSpec as P

BX = 8
BY = 128
SWEEPS = 2


def padded_2(block, sides, width):
    for axis, dim in sides:
        count = lax.axis_size(axis)
        forward = [(i, i + 1) for i in range(count - 1)]
        backward = [(target, source) for source, target in forward]
        low = lax.ppermute(
            lax.slice_in_dim(block, block.shape[dim] - width, None, axis=dim), axis, forward
        )
        high = lax.ppermute(lax.slice_in_dim(block, 0, width, axis=dim), axis, backward)
        block = jnp.concatenate([low, block, high], axis=dim)
    return block


def passed_along(value, axis, steps):
    count = lax.axis_size(axis)
    first, last = (max(0, -steps), min(count, count - steps))
    return lax.ppermute(value, axis, [(source, source + steps) for source in range(first, last)])


def directions(wind_codes):
    per_cell = jnp.repeat(jnp.repeat(wind_codes, BX, axis=1), BY, axis=2)
    side_rows = 1 - 2 * (per_cell % 2)
    side_cols = 1 - 2 * (per_cell // 2)
    return (side_rows, side_cols)


def advance(values_in, side_rows, side_cols, courant_rows, courant_cols):
    padded = padded_2(values_in, (("space", 1),), 1)
    from_rows = jnp.where(side_rows > 0, padded[:, :-2], padded[:, 2:])
    from_cols = jnp.where(
        side_cols > 0, jnp.roll(values_in, 1, axis=2), jnp.roll(values_in, -1, axis=2)
    )
    return (
        (1.0 - courant_rows - courant_cols) * values_in
        + courant_rows * from_rows
        + courant_cols * from_cols
    )


def smooth(values_in):
    slab_rows = values_in.shape[1]
    total_rows = slab_rows * lax.axis_size("space")
    first_row = lax.axis_index("space") * slab_rows
    field = padded_2(values_in, (("space", 1),), SWEEPS)
    for sweep in range(SWEEPS):
        margin = SWEEPS - 1 - sweep
        middle = field[:, 1:-1]
        beside_all = (
            field[:, :-2]
            + field[:, 2:]
            + jnp.roll(middle, 1, axis=2)
            + jnp.roll(middle, -1, axis=2)
        )
        updated = middle + 0.2 * (beside_all - 4.0 * middle)
        global_rows = first_row - margin + jnp.arange(updated.shape[1], dtype=jnp.int32)
        inside = (global_rows >= 0) & (global_rows < total_rows)
        field = jnp.where(inside[None, :, None], updated, 0.0)
    return field


def retreat(values_in, side_rows, side_cols, courant_rows, courant_cols):
    along_rows = courant_rows * values_in
    pieces = jnp.stack(
        [jnp.where(side_rows > 0, along_rows, 0.0), jnp.where(side_rows < 0, along_rows, 0.0)],
        axis=1,
    )
    downward = pieces[:, 0]
    upward = pieces[:, 1]
    from_above = passed_along(downward[:, :1], "space", -1)
    from_below = passed_along(upward[:, -1:], "space", 1)
    from_rows = jnp.concatenate([downward[:, 1:], from_above], axis=1) + jnp.concatenate(
        [from_below, upward[:, :-1]], axis=1
    )
    along_cols = courant_cols * values_in
    plus_cols = jnp.where(side_cols > 0, along_cols, 0.0)
    minus_cols = jnp.where(side_cols < 0, along_cols, 0.0)
    from_cols = jnp.roll(plus_cols, -1, axis=2) + jnp.roll(minus_cols, 1, axis=2)
    return (1.0 - courant_rows - courant_cols) * values_in + from_rows + from_cols


def on_device(increments, precision, courant_rows, courant_cols, wind_codes):
    incoming = passed_along(increments[1], "tm", 1)
    side_rows, side_cols = directions(wind_codes)
    inputs = jnp.stack([incoming, increments[0]])
    moved = advance(inputs, side_rows, side_cols, courant_rows, courant_cols)
    misfit = increments - moved
    weighted = smooth(precision * smooth(misfit))
    images = retreat(weighted, side_rows, side_cols, courant_rows, courant_cols)
    from_next = passed_along(images[0], "tm", -1)
    adjoint_image = jnp.stack([weighted[0] - images[1], weighted[1] - from_next])
    return (misfit, adjoint_image)


def solution(mesh):
    in_specs = (
        P("tm", "space", None),
        P("tm", "space", None),
        P("space", None),
        P("space", None),
        P("tm", "space", None),
    )
    out_specs = (P("tm", "space", None), P("tm", "space", None))
    return jax.shard_map(
        on_device, mesh=mesh, in_specs=in_specs, out_specs=out_specs, check_vma=False
    )
```

profile of v0, /device:TPU:1, one launch (start us, length us, event | category | flops | bytes accessed | tf_op | source)
XLA Modules:
  0.0 71.9 jit_solution(5217755625234251903)
XLA Ops:
  0.6 0.0 copy-start
  0.6 2.1 %slice_bitcast_fusion.2 = (f32[64,2048]{1,0:T(8,128)}, f32[1,64,2048]{2,1,0:T(8,128)S(1)}) fusion(f32[2,64,2048]{2,1,0:T(8,128)} %param.5), kind=kLoop, calls=%fused_computation.98 | loop fusion | bytes 2097152 | tf_op jit(solution)/shard_map/squeeze | solution.py:92
  2.7 4.5 %collective-permute-start = (f32[64,2048]{1,0:T(8,128)}, f32[64,2048]{1,0:T(8,128)S(1)}, u32[]{:S(2)}, u32[]{:S(2)}) collective-permute-start(f32[64,2048]{1,0:T(8,128)} %get-tuple-element.31), channel_id=1, source_target_pairs={{0,4},{4,8},{8,12},{12,16},{16,20},{20,24},{24,28},{1,5},{5,9},{9,... | collective-permute-start | bytes 1572872 | tf_op jit(solution)/shard_map/ppermute | solution.py:27
  7.3 1.3 %broadcast_in_dim.54 = s32[2,64,16,128]{3,2,1,0:T(8,128)} broadcast(s32[2,64,16]{2,1,0:T(8,128)S(1)} %broadcast_bitcast_fusion), dimensions={0,1,2} | broadcast | bytes 1056768 | tf_op jit(solution)/shard_map/broadcast_in_dim | solution.py:31
  8.6 1.5 %reshape.28 = s32[2,64,2048]{2,1,0:T(8,128)S(1)} reshape(s32[2,64,16,128]{3,2,1,0:T(8,128)} %broadcast_in_dim.54) | data formatting | bytes 2097152 | tf_op jit(solution)/shard_map/reshape | solution.py:31
  10.0 0.0 copy-done.3
  10.1 0.1 subtract_subtract_fusion
  10.1 3.5 %collective-permute-done = f32[64,2048]{1,0:T(8,128)S(1)} collective-permute-done((f32[64,2048]{1,0:T(8,128)}, f32[64,2048]{1,0:T(8,128)S(1)}, u32[]{:S(2)}, u32[]{:S(2)}) %collective-permute-start) | collective-permute-done | bytes 524320 | tf_op jit(solution)/shard_map/ppermute | solution.py:27
  13.7 0.4 fusion.21
  14.0 0.0 copy-start.4
  14.0 3.3 %collective-permute-start.1 = (f32[2,1,2048]{2,1,0:T(1,128)S(1)}, f32[2,1,2048]{2,1,0:T(1,128)S(1)}, u32[]{:S(2)}, u32[]{:S(2)}) collective-permute-start(f32[2,1,2048]{2,1,0:T(1,128)S(1)} %get-tuple-element.29), channel_id=1, source_target_pairs={{0,1},{1,2},{2,3},{4,5},{5,6},{6,7},{8,9},{9,10},{10,11},{12,13},{... | collective-permute-start | bytes 49160 | tf_op jit(solution)/shard_map/ppermute | solution.py:16
  17.4 1.3 %collective-permute-start.2 = (f32[2,1,2048]{2,1,0:T(1,128)S(1)}, f32[2,1,2048]{2,1,0:T(1,128)S(1)}, u32[]{:S(2)}, u32[]{:S(2)}) collective-permute-start(f32[2,1,2048]{2,1,0:T(1,128)S(1)} %get-tuple-element.30), channel_id=1, source_target_pairs={{1,0},{2,1},{3,2},{5,4},{6,5},{7,6},{9,8},{10,9},{11,10},{13,12},{... | collective-permute-start | bytes 49160 | tf_op jit(solution)/shard_map/ppermute | solution.py:19
  18.7 0.1 fusion.49
  18.8 3.1 %collective-permute-done.2 = f32[2,1,2048]{2,1,0:T(1,128)S(1)} collective-permute-done((f32[2,1,2048]{2,1,0:T(1,128)S(1)}, f32[2,1,2048]{2,1,0:T(1,128)S(1)}, u32[]{:S(2)}, u32[]{:S(2)}) %collective-permute-start.2) | collective-permute-done | bytes 16416 | tf_op jit(solution)/shard_map/ppermute | solution.py:19
  21.9 2.0 %fusion.25 = f32[2,64,2048]{2,1,0:T(8,128)S(1)} fusion(f32[2,64,2048]{2,1,0:T(8,128)S(1)} %copy-done.4, f32[1,64,2048]{2,1,0:T(8,128)S(1)} %get-tuple-element.32, f32[1,64,2048]{2,1,0:T(8,128)S(1)} %bitcast.22, f32[2,1,2048]{2,1,0:T(1,128)S(1)} %collective-permute-done.2, f32[2,1,2048]{2,1,0:T(1,128)S(1)} %collective-permute-done.1, ...), kind=kLoop, calls=%fused_computation.55 | loop fusion | flops 10485760 | bytes 7897088 | tf_op jit(solution)/shard_map/sub | solution.py:96
  23.9 3.2 %collective-permute-start.3 = (f32[2,2,2048]{2,1,0:T(2,128)S(1)}, f32[2,2,2048]{2,1,0:T(2,128)S(1)}, u32[]{:S(2)}, u32[]{:S(2)}) collective-permute-start(f32[2,2,2048]{2,1,0:T(2,128)S(1)} %get-tuple-element.23), channel_id=1, source_target_pairs={{0,1},{1,2},{2,3},{4,5},{5,6},{6,7},{8,9},{9,10},{10,11},{12,13},{... | collective-permute-start | bytes 98312 | tf_op jit(solution)/shard_map/ppermute | solution.py:16
  27.1 1.3 %collective-permute-start.4 = (f32[2,2,2048]{2,1,0:T(2,128)S(1)}, f32[2,2,2048]{2,1,0:T(2,128)S(1)}, u32[]{:S(2)}, u32[]{:S(2)}) collective-permute-start(f32[2,2,2048]{2,1,0:T(2,128)S(1)} %get-tuple-element.24), channel_id=1, source_target_pairs={{1,0},{2,1},{3,2},{5,4},{6,5},{7,6},{9,8},{10,9},{11,10},{13,12},{... | collective-permute-start | bytes 98312 | tf_op jit(solution)/shard_map/ppermute | solution.py:19
  28.4 3.3 %collective-permute-done.4 = f32[2,2,2048]{2,1,0:T(2,128)S(1)} collective-permute-done((f32[2,2,2048]{2,1,0:T(2,128)S(1)}, f32[2,2,2048]{2,1,0:T(2,128)S(1)}, u32[]{:S(2)}, u32[]{:S(2)}) %collective-permute-start.4) | collective-permute-done | bytes 32800 | tf_op jit(solution)/shard_map/ppermute | solution.py:19
  31.7 0.2 pad_maximum_fusion.9
  31.9 0.4 fusion.58
  32.4 0.7 %fusion.13 = f32[2,66,2048]{2,1,0:T(8,128)S(1)} fusion(f32[2,2,2048]{2,1,0:T(2,128)S(1)} %collective-permute-done.4, f32[2,64,2048]{2,1,0:T(8,128)S(1)} %fusion.25, f32[2,2,2048]{2,1,0:T(2,128)S(1)} %collective-permute-done.3, f32[2,66,2047]{2,1,0:T(8,128)S(1)} %get-tuple-element.18, f32[2,66,2047]{2,1,0:T(8,128)S(1)} %get-tuple-element.17, ...), kind=kLoop, calls=%fused_computation.36 | loop fusion | flops 4325376 | bytes 5438498 | tf_op jit(solution)/shard_map/jit(_where)/select_n | solution.py:67
  33.1 0.1 fusion.57
  33.2 0.0 copy-start.5
  33.2 0.4 fusion.56
  33.6 0.8 %copy-done.5 = f32[2,64,2048]{2,1,0:T(8,128)S(1)} copy-done((f32[2,64,2048]{2,1,0:T(8,128)S(1)}, f32[2,64,2048]{2,1,0:T(8,128)}, u32[]{:S(2)}) %copy-start.5) | copy-done | bytes 1048600
  34.4 0.6 fusion.38
  35.1 3.2 %collective-permute-start.5 = (f32[2,2,2048]{2,1,0:T(2,128)S(1)}, f32[2,2,2048]{2,1,0:T(2,128)S(1)}, u32[]{:S(2)}, u32[]{:S(2)}) collective-permute-start(f32[2,2,2048]{2,1,0:T(2,128)S(1)} %get-tuple-element.21), channel_id=1, source_target_pairs={{0,1},{1,2},{2,3},{4,5},{5,6},{6,7},{8,9},{9,10},{10,11},{12,13},{... | collective-permute-start | bytes 98312 | tf_op jit(solution)/shard_map/ppermute | solution.py:16
  38.3 1.3 %collective-permute-start.6 = (f32[2,2,2048]{2,1,0:T(2,128)S(1)}, f32[2,2,2048]{2,1,0:T(2,128)S(1)}, u32[]{:S(2)}, u32[]{:S(2)}) collective-permute-start(f32[2,2,2048]{2,1,0:T(2,128)S(1)} %get-tuple-element.22), channel_id=1, source_target_pairs={{1,0},{2,1},{3,2},{5,4},{6,5},{7,6},{9,8},{10,9},{11,10},{13,12},{... | collective-permute-start | bytes 98312 | tf_op jit(solution)/shard_map/ppermute | solution.py:19
  39.6 3.3 %collective-permute-done.6 = f32[2,2,2048]{2,1,0:T(2,128)S(1)} collective-permute-done((f32[2,2,2048]{2,1,0:T(2,128)S(1)}, f32[2,2,2048]{2,1,0:T(2,128)S(1)}, u32[]{:S(2)}, u32[]{:S(2)}) %collective-permute-start.6) | collective-permute-done | bytes 32800 | tf_op jit(solution)/shard_map/ppermute | solution.py:19
  42.9 0.1 pad_maximum_fusion.10
  43.1 0.4 fusion.55
  43.5 0.7 %fusion.5 = f32[2,66,2048]{2,1,0:T(8,128)S(1)} fusion(f32[2,2,2048]{2,1,0:T(2,128)S(1)} %collective-permute-done.6, f32[2,64,2048]{2,1,0:T(8,128)S(1)} %fusion.38, f32[2,2,2048]{2,1,0:T(2,128)S(1)} %collective-permute-done.5, f32[2,66,2047]{2,1,0:T(8,128)S(1)} %get-tuple-element.12, f32[2,66,2047]{2,1,0:T(8,128)S(1)} %get-tuple-element.11, ...), kind=kLoop, calls=%fused_computation.24 | loop fusion | flops 4325376 | bytes 5438498 | tf_op jit(solution)/shard_map/jit(_where)/select_n | solution.py:67
  44.2 0.1 fusion.53
  44.3 0.4 fusion.54
  44.7 1.2 %compare_select_fusion = (f32[2,64,2048]{2,1,0:T(8,128)S(1)}, f32[2,64,2048]{2,1,0:T(8,128)S(1)}) fusion(f32[64,2048]{1,0:T(8,128)S(1)} %copy-done.2, s32[2,64,2048]{2,1,0:T(8,128)S(1)} %reshape.28, f32[2,64,1]{2,1,0:T(8,128)S(1)} %get-tuple-element.8, f32[2,64,2047]{2,1,0:T(8,128)S(1)} %get-tuple-element.10, f32[2,64,2047]{2,1,0:T(8,128)S(1)} %get-tuple-element.9, ...), kind=kLoop, calls=%fused_computation.86 | loop fusion | flops 7864320 | bytes 8912960 | tf_op jit(solution)/shard_map/jit(_where)/select_n | solution.py:86
  45.9 1.3 %compare_select_fusion.1 = (f32[2,64,2048]{2,1,0:T(8,128)S(1)}, f32[2,64,2048]{2,1,0:T(8,128)S(1)}, f32[2,64,2048]{2,1,0:T(8,128)S(1)}) fusion(f32[2,64,2048]{2,1,0:T(8,128)S(1)} %get-tuple-element.3, f32[64,2048]{1,0:T(8,128)S(1)} %copy-done.3, s32[2,64,2048]{2,1,0:T(8,128)S(1)} %reshape.28, f32[64,2048]{1,0:T(8,128)S(1)} %copy-done.2), kind=kLoop, calls=%fused_computation.87 | loop fusion | flops 8126464 | bytes 6291456 | tf_op jit(solution)/shard_map/jit(_where)/select_n | solution.py:74
  47.3 1.3 %collective-permute-start.7 = (f32[2,1,2048]{2,1,0:T(1,128)S(1)}, f32[2,1,2048]{2,1,0:T(1,128)S(1)}, u32[]{:S(2)}, u32[]{:S(2)}) collective-permute-start(f32[2,1,2048]{2,1,0:T(1,128)S(1)} %slice.272), channel_id=1, source_target_pairs={{1,0},{2,1},{3,2},{5,4},{6,5},{7,6},{9,8},{10,9},{11,10},{13,12},{... | collective-permute-start | bytes 49160 | tf_op jit(solution)/shard_map/ppermute | solution.py:27
  48.6 4.0 %collective-permute-start.8 = (f32[2,1,2048]{2,1,0:T(1,128)S(1)}, f32[2,1,2048]{2,1,0:T(1,128)S(1)}, u32[]{:S(2)}, u32[]{:S(2)}) collective-permute-start(f32[2,1,2048]{2,1,0:T(1,128)S(1)} %slice.273), channel_id=1, source_target_pairs={{0,1},{1,2},{2,3},{4,5},{5,6},{6,7},{8,9},{9,10},{10,11},{12,13},{... | collective-permute-start | bytes 49160 | tf_op jit(solution)/shard_map/ppermute | solution.py:27
  52.6 0.1 slice.271
  52.7 0.3 slice.275
  53.0 0.1 slice.277
  53.1 0.3 collective-permute-done.8
  53.4 0.7 fusion.43
  54.1 0.1 slice_subtract_fusion
  54.2 2.6 %collective-permute-start.9 = (f32[64,2048]{1,0:T(8,128)S(1)}, f32[64,2048]{1,0:T(8,128)S(1)}, u32[]{:S(2)}, u32[]{:S(2)}) collective-permute-start(f32[64,2048]{1,0:T(8,128)S(1)} %get-tuple-element.20), channel_id=1, source_target_pairs={{4,0},{8,4},{12,8},{16,12},{20,16},{24,20},{28,24},{5,1},{9,5},{13... | collective-permute-start | bytes 1572872 | tf_op jit(solution)/shard_map/ppermute | solution.py:27
  56.9 13.9 %collective-permute-done.9 = f32[64,2048]{1,0:T(8,128)S(1)} collective-permute-done((f32[64,2048]{1,0:T(8,128)S(1)}, f32[64,2048]{1,0:T(8,128)S(1)}, u32[]{:S(2)}, u32[]{:S(2)}) %collective-permute-start.9) | collective-permute-done | bytes 524320 | tf_op jit(solution)/shard_map/ppermute | solution.py:27
  70.8 0.1 fusion.47
  70.9 1.0 %pad_maximum_fusion.15 = f32[2,64,2048]{2,1,0:T(8,128)} fusion(f32[1,64,2048]{2,1,0:T(8,128)S(1)} %fusion.47, f32[1,64,2048]{2,1,0:T(8,128)S(1)} %get-tuple-element.19), kind=kLoop, calls=%fused_computation.83 | loop fusion | flops 262144 | bytes 2097152 | tf_op jit(solution)/shard_map/stack | solution.py:100
  (20 shorter events, 0.2 us)
Async XLA Ops:
  0.6 6.6 %copy-start = (s32[2,8,16]{2,1,0:T(8,128)S(1)}, s32[2,8,16]{2,1,0:T(8,128)}, u32[]{:S(2)}) copy-start(s32[2,8,16]{2,1,0:T(8,128)} %param.9) | copy-start | bytes 3076
  2.7 10.9 %collective-permute-start = (f32[64,2048]{1,0:T(8,128)}, f32[64,2048]{1,0:T(8,128)S(1)}, u32[]{:S(2)}, u32[]{:S(2)}) collective-permute-start(f32[64,2048]{1,0:T(8,128)} %get-tuple-element.31), channel_id=1, source_target_pairs={{0,4},{4,8},{8,12},{12,16},{16,20},{20,24},{24,28},{1,5},{5,9},{9,... | collective-permute-start | bytes 1572872 | tf_op jit(solution)/shard_map/ppermute | solution.py:27
  8.6 1.5 %copy-start.2 = (f32[64,2048]{1,0:T(8,128)S(1)}, f32[64,2048]{1,0:T(8,128)}, u32[]{:S(2)}) copy-start(f32[64,2048]{1,0:T(8,128)} %param.8) | copy-start | bytes 1572868
  8.6 1.5 %copy-start.3 = (f32[64,2048]{1,0:T(8,128)S(1)}, f32[64,2048]{1,0:T(8,128)}, u32[]{:S(2)}) copy-start(f32[64,2048]{1,0:T(8,128)} %param.7) | copy-start | bytes 1572868
  14.0 7.8 %copy-start.4 = (f32[2,64,2048]{2,1,0:T(8,128)S(1)}, f32[2,64,2048]{2,1,0:T(8,128)}, u32[]{:S(2)}) copy-start(f32[2,64,2048]{2,1,0:T(8,128)} %param.5) | copy-start | bytes 3145732
  14.0 4.7 %collective-permute-start.1 = (f32[2,1,2048]{2,1,0:T(1,128)S(1)}, f32[2,1,2048]{2,1,0:T(1,128)S(1)}, u32[]{:S(2)}, u32[]{:S(2)}) collective-permute-start(f32[2,1,2048]{2,1,0:T(1,128)S(1)} %get-tuple-element.29), channel_id=1, source_target_pairs={{0,1},{1,2},{2,3},{4,5},{5,6},{6,7},{8,9},{9,10},{10,11},{12,13},{... | collective-permute-start | bytes 49160 | tf_op jit(solution)/shard_map/ppermute | solution.py:16
  17.4 4.5 %collective-permute-start.2 = (f32[2,1,2048]{2,1,0:T(1,128)S(1)}, f32[2,1,2048]{2,1,0:T(1,128)S(1)}, u32[]{:S(2)}, u32[]{:S(2)}) collective-permute-start(f32[2,1,2048]{2,1,0:T(1,128)S(1)} %get-tuple-element.30), channel_id=1, source_target_pairs={{1,0},{2,1},{3,2},{5,4},{6,5},{7,6},{9,8},{10,9},{11,10},{13,12},{... | collective-permute-start | bytes 49160 | tf_op jit(solution)/shard_map/ppermute | solution.py:19
  23.8 8.5 %copy-start.1 = (f32[2,64,2048]{2,1,0:T(8,128)}, f32[2,64,2048]{2,1,0:T(8,128)S(1)}, u32[]{:S(2)}) copy-start(f32[2,64,2048]{2,1,0:T(8,128)S(1)} %fusion.25) | copy-start | bytes 3145732
  23.9 4.5 %collective-permute-start.3 = (f32[2,2,2048]{2,1,0:T(2,128)S(1)}, f32[2,2,2048]{2,1,0:T(2,128)S(1)}, u32[]{:S(2)}, u32[]{:S(2)}) collective-permute-start(f32[2,2,2048]{2,1,0:T(2,128)S(1)} %get-tuple-element.23), channel_id=1, source_target_pairs={{0,1},{1,2},{2,3},{4,5},{5,6},{6,7},{8,9},{9,10},{10,11},{12,13},{... | collective-permute-start | bytes 98312 | tf_op jit(solution)/shard_map/ppermute | solution.py:16
  27.1 4.7 %collective-permute-start.4 = (f32[2,2,2048]{2,1,0:T(2,128)S(1)}, f32[2,2,2048]{2,1,0:T(2,128)S(1)}, u32[]{:S(2)}, u32[]{:S(2)}) collective-permute-start(f32[2,2,2048]{2,1,0:T(2,128)S(1)} %get-tuple-element.24), channel_id=1, source_target_pairs={{1,0},{2,1},{3,2},{5,4},{6,5},{7,6},{9,8},{10,9},{11,10},{13,12},{... | collective-permute-start | bytes 98312 | tf_op jit(solution)/shard_map/ppermute | solution.py:19
  33.2 1.2 %copy-start.5 = (f32[2,64,2048]{2,1,0:T(8,128)S(1)}, f32[2,64,2048]{2,1,0:T(8,128)}, u32[]{:S(2)}) copy-start(f32[2,64,2048]{2,1,0:T(8,128)} %param.6) | copy-start | bytes 3145732
  35.1 4.5 %collective-permute-start.5 = (f32[2,2,2048]{2,1,0:T(2,128)S(1)}, f32[2,2,2048]{2,1,0:T(2,128)S(1)}, u32[]{:S(2)}, u32[]{:S(2)}) collective-permute-start(f32[2,2,2048]{2,1,0:T(2,128)S(1)} %get-tuple-element.21), channel_id=1, source_target_pairs={{0,1},{1,2},{2,3},{4,5},{5,6},{6,7},{8,9},{9,10},{10,11},{12,13},{... | collective-permute-start | bytes 98312 | tf_op jit(solution)/shard_map/ppermute | solution.py:16
  38.3 4.7 %collective-permute-start.6 = (f32[2,2,2048]{2,1,0:T(2,128)S(1)}, f32[2,2,2048]{2,1,0:T(2,128)S(1)}, u32[]{:S(2)}, u32[]{:S(2)}) collective-permute-start(f32[2,2,2048]{2,1,0:T(2,128)S(1)} %get-tuple-element.22), channel_id=1, source_target_pairs={{1,0},{2,1},{3,2},{5,4},{6,5},{7,6},{9,8},{10,9},{11,10},{13,12},{... | collective-permute-start | bytes 98312 | tf_op jit(solution)/shard_map/ppermute | solution.py:19
  47.3 5.8 %collective-permute-start.7 = (f32[2,1,2048]{2,1,0:T(1,128)S(1)}, f32[2,1,2048]{2,1,0:T(1,128)S(1)}, u32[]{:S(2)}, u32[]{:S(2)}) collective-permute-start(f32[2,1,2048]{2,1,0:T(1,128)S(1)} %slice.272), channel_id=1, source_target_pairs={{1,0},{2,1},{3,2},{5,4},{6,5},{7,6},{9,8},{10,9},{11,10},{13,12},{... | collective-permute-start | bytes 49160 | tf_op jit(solution)/shard_map/ppermute | solution.py:27
  48.6 4.8 %collective-permute-start.8 = (f32[2,1,2048]{2,1,0:T(1,128)S(1)}, f32[2,1,2048]{2,1,0:T(1,128)S(1)}, u32[]{:S(2)}, u32[]{:S(2)}) collective-permute-start(f32[2,1,2048]{2,1,0:T(1,128)S(1)} %slice.273), channel_id=1, source_target_pairs={{0,1},{1,2},{2,3},{4,5},{5,6},{6,7},{8,9},{9,10},{10,11},{12,13},{... | collective-permute-start | bytes 49160 | tf_op jit(solution)/shard_map/ppermute | solution.py:27
  54.2 16.6 %collective-permute-start.9 = (f32[64,2048]{1,0:T(8,128)S(1)}, f32[64,2048]{1,0:T(8,128)S(1)}, u32[]{:S(2)}, u32[]{:S(2)}) collective-permute-start(f32[64,2048]{1,0:T(8,128)S(1)} %get-tuple-element.20), channel_id=1, source_target_pairs={{4,0},{8,4},{12,8},{16,12},{20,16},{24,20},{28,24},{5,1},{9,5},{13... | collective-permute-start | bytes 1572872 | tf_op jit(solution)/shard_map/ppermute | solution.py:27
where the time goes:
time: 73.2 us; the launch traced here: 71.9 us
  waiting for transfers between devices  27.5 us (38%)
  starting transfers between devices  26 us (36%)
  other arithmetic  9.29 us (13%)
  local copies, waits for them, and re-layouts  8.12 us (11%)
  between operations  0.98 us (1%)
    ppermute x4, waiting for transfers between devices, passed_along(): lax.ppermute(value, axis, [(source, source + steps) for source in range(f...  17.7 us
    ppermute x4, starting transfers between devices, passed_along(): lax.ppermute(value, axis, [(source, source + steps) for source in range(f...  12.4 us
    ppermute x3, waiting for transfers between devices, padded_2(): lax.ppermute(lax.slice_in_dim(block, 0, width, axis=dim), axis, backward)  9.78 us
    ppermute x3, starting transfers between devices, padded_2(): lax.ppermute(lax.slice_in_dim(block, block.shape[dim] - width, None, axis...  9.74 us
    ppermute x3, starting transfers between devices, padded_2(): lax.ppermute(lax.slice_in_dim(block, 0, width, axis=dim), axis, backward)  3.88 us
    squeeze x1, local copies, waits for them, and re-layouts, on_device(): incoming = passed_along(increments[1], 'tm', 1)  2.07 us
    sub x1, other arithmetic, on_device(): misfit = increments - moved  1.95 us
    reshape x2, local copies, waits for them, and re-layouts, directions(): per_cell = jnp.repeat(jnp.repeat(wind_codes, BX, axis=1), BY, axis=2)  1.48 us
  transfers between devices with their start and end apart: 10, of which 6 were waited for; matrix products, arithmetic and copies ran while one was open for 5% of the time, Pallas kernels for 0%

commit v1 on v0

v1 whole, which is shorter than its diff:
```python
import functools

import jax
import jax.numpy as jnp
from jax import lax
from jax.experimental import pallas as pl
from jax.experimental.pallas import tpu as pltpu
from jax.sharding import PartitionSpec as P

BX = 8
BY = 128
SWEEPS = 2
CHUNKS = 4
MESH = pl.DeviceIdType.MESH


def kernel(
    inc, prec, crow, ccol, codes,
    misfit_out, adjoint_out,
    incx, precx, cx, codex, cexp, ms, fa, fb, w, dn, up_, img, back, adj,
    local_sem, out_sem, zsend, zrecv, tsend, trecv, bsend, brecv,
):
    rows, cols = crow.shape
    blocks = rows // BX
    ext = rows + 2 * BX
    s = lax.axis_index("space")
    t = lax.axis_index("tm")
    n_s = lax.axis_size("space")
    n_t = lax.axis_size("tm")
    has_lo, has_hi = s > 0, s < n_s - 1
    has_prev, has_next = t > 0, t < n_t - 1
    own = pl.ds(BX, rows)
    top = pl.ds(0, BX)
    bottom = pl.ds(BX + rows, BX)
    first = pl.ds(0, BX)
    last = pl.ds(rows - BX, BX)
    chunk = rows // CHUNKS

    neighbours = (
        (has_lo, {"space": s - 1}),
        (has_hi, {"space": s + 1}),
        (has_prev, {"tm": t - 1}),
        (has_next, {"tm": t + 1}),
    )

    loads = [
        pltpu.make_async_copy(inc, incx.at[pl.ds(1, 2), own], local_sem.at[0]),
        pltpu.make_async_copy(crow, cx.at[0, own], local_sem.at[1]),
        pltpu.make_async_copy(ccol, cx.at[1, own], local_sem.at[2]),
        pltpu.make_async_copy(codes, codex.at[1], local_sem.at[3]),
        pltpu.make_async_copy(prec, precx.at[:, own], local_sem.at[4]),
    ]
    for load in loads:
        load.start()

    barrier = pltpu.get_barrier_semaphore()
    for there, where in neighbours:
        @pl.when(there)
        def _(where=where):
            pl.semaphore_signal(barrier, inc=1, device_id=where, device_id_type=MESH)
    count = sum(there.astype(jnp.int32) for there, _ in neighbours)
    pl.semaphore_wait(barrier, count)

    def remote(src, dst, send, recv, where):
        return pltpu.make_async_remote_copy(
            src_ref=src, dst_ref=dst, send_sem=send, recv_sem=recv,
            device_id=where, device_id_type=MESH,
        )

    def z_copies(side):
        edge = first if side == 0 else last
        halo = bottom if side == 0 else top
        where = {"space": s - 1} if side == 0 else {"space": s + 1}
        pairs = [
            (inc.at[:, edge], incx.at[pl.ds(1, 2), halo]),
            (crow.at[edge], cx.at[0, halo]),
            (ccol.at[edge], cx.at[1, halo]),
            (codes, codex.at[2 if side == 0 else 0]),
            (prec.at[:, edge], precx.at[:, halo]),
        ]
        return [
            remote(src, dst, zsend.at[side, i], zrecv.at[side, i], where)
            for i, (src, dst) in enumerate(pairs)
        ]

    forward = remote(inc.at[1], incx.at[0, own], tsend.at[0], trecv.at[0], {"tm": t + 1})
    relay_top = remote(incx.at[2, top], incx.at[0, top], tsend.at[1], trecv.at[1], {"tm": t + 1})
    relay_bottom = remote(incx.at[2, bottom], incx.at[0, bottom], tsend.at[2], trecv.at[2], {"tm": t + 1})

    def back_copy(i):
        part = pl.ds(i * chunk, chunk)
        return remote(img.at[0, part], back.at[part], bsend.at[i], brecv.at[i], {"tm": t - 1})

    @pl.when(has_next)
    def _():
        forward.start()

    sent_to = ((0, has_lo), (1, has_hi))
    arrives = ((0, has_hi), (1, has_lo))
    to_side = {0: z_copies(0), 1: z_copies(1)}
    for i in range(5):
        for side, there in sent_to:
            @pl.when(there)
            def _(side=side, i=i):
                to_side[side][i].start()

    def clear(ref_rows):
        for k in range(3):
            incx[k, ref_rows, :] = jnp.zeros((BX, cols), jnp.float32)
        for k in range(2):
            precx[k, ref_rows, :] = jnp.zeros((BX, cols), jnp.float32)
            cx[k, ref_rows, :] = jnp.zeros((BX, cols), jnp.float32)

    @pl.when(jnp.logical_not(has_lo))
    def _():
        clear(top)
        codex[0] = jnp.zeros(codex.shape[1:], jnp.int32)

    @pl.when(jnp.logical_not(has_hi))
    def _():
        clear(bottom)
        codex[2] = jnp.zeros(codex.shape[1:], jnp.int32)

    @pl.when(jnp.logical_not(has_prev))
    def _():
        incx[0] = jnp.zeros((ext, cols), jnp.float32)

    @pl.when(jnp.logical_not(has_next))
    def _():
        back[...] = jnp.zeros((rows, cols), jnp.float32)

    def arrived(i):
        for side, there in arrives:
            @pl.when(there)
            def _(side=side):
                to_side[side][i].wait_recv()

    loads[0].wait()
    arrived(0)

    @pl.when(has_next & has_lo)
    def _():
        relay_top.start()

    @pl.when(has_next & has_hi)
    def _():
        relay_bottom.start()

    for i in (1, 2, 3):
        loads[i].wait()
        arrived(i)

    for part in range(3):
        for k in range(2):
            value = codex[part, k]
            for j in range(cols // BY):
                cexp[k, pl.ds(part * blocks, blocks), pl.ds(j * BY, BY)] = jnp.broadcast_to(
                    value[:, j : j + 1], (blocks, BY)
                )

    row = lax.broadcasted_iota(jnp.int32, (BX, cols), 0)
    is_first, is_last = row == 0, row == BX - 1

    def at(b):
        return pl.ds(pl.multiple_of(b * BX, BX), BX)

    def above(ref, k, b, cur):
        prev = ref[k, at(jnp.maximum(b - 1, 0)), :]
        return pltpu.roll(jnp.where(is_last, prev, cur), 1, 0)

    def below(ref, k, b, cur):
        after = ref[k, at(jnp.minimum(b + 1, blocks + 1)), :]
        return pltpu.roll(jnp.where(is_first, after, cur), BX - 1, 0)

    def left(cur):
        return pltpu.roll(cur, 1, 1)

    def right(cur):
        return pltpu.roll(cur, cols - 1, 1)

    def inside(b, value):
        keep = ((b > 0) | has_lo) & ((b < blocks + 1) | has_hi)
        return jnp.where(keep, value, 0.0)

    def code_of(k, b):
        return jnp.broadcast_to(cexp[k, pl.ds(b + blocks - 1, 1), :], (BX, cols))

    def star(ref, k, b):
        cur = ref[k, at(b), :]
        return cur + above(ref, k, b, cur) + below(ref, k, b, cur) + (left(cur) + right(cur))

    def misfits(k):
        def body(b, carry):
            cur = incx[k, at(b), :]
            code = code_of(k, b)
            from_rows = jnp.where(code % 2 == 0, above(incx, k, b, cur), below(incx, k, b, cur))
            from_cols = jnp.where(code < 2, left(cur), right(cur))
            moved = cur + cx[0, at(b), :] * (from_rows - cur) + cx[1, at(b), :] * (from_cols - cur)
            ms[k, at(b), :] = inside(b, incx[k + 1, at(b), :] - moved)
            return carry

        lax.fori_loop(0, blocks + 2, body, 0)

    def sweep(src, dst, k, scale=None):
        def body(b, carry):
            value = star(src, k, b)
            if scale is not None:
                value = scale[k, at(b), :] * value
            dst[k, at(b), :] = inside(b, value)
            return carry

        lax.fori_loop(0, blocks + 2, body, 0)

    def weigh(k):
        def body(b, carry):
            value = inside(b, star(fa, k, b) * (0.2 ** (2 * SWEEPS)))
            code = code_of(k, b)
            along = cx[0, at(b), :] * value
            w[k, at(b), :] = value
            dn[k, at(b), :] = jnp.where(code % 2 == 0, along, 0.0)
            up_[k, at(b), :] = jnp.where(code % 2 == 0, 0.0, along)
            return carry

        lax.fori_loop(0, blocks + 2, body, 0)

    def retreat(k, start, stop):
        def body(b, carry):
            value = w[k, at(b), :]
            code = code_of(k, b)
            d, u = dn[k, at(b), :], up_[k, at(b), :]
            cols_part = cx[1, at(b), :] * value
            plus = jnp.where(code < 2, cols_part, 0.0)
            minus = cols_part - plus
            image = (
                value - (d + u) - cols_part
                + below(dn, k, b, d) + above(up_, k, b, u)
                + right(plus) + left(minus)
            )
            img[k, at(b - 1), :] = image
            if k == 0:
                adj[0, at(b - 1), :] = value - img[1, at(b - 1), :]
            return carry

        lax.fori_loop(start, stop, body, 0)

    misfit_copies = [
        pltpu.make_async_copy(ms.at[k, own], misfit_out.at[k], out_sem.at[k]) for k in range(2)
    ]

    def half_one(k):
        misfits(k)
        misfit_copies[k].start()
        sweep(ms, fa, k)

    def half_two(k):
        sweep(fa, fb, k, precx)
        sweep(fb, fa, k)
        weigh(k)

    half_one(1)
    loads[4].wait()
    arrived(4)
    half_two(1)
    retreat(1, 1, blocks + 1)

    @pl.when(has_prev)
    def _():
        forward.wait_recv()

    @pl.when(has_prev & has_lo)
    def _():
        relay_top.wait_recv()

    @pl.when(has_prev & has_hi)
    def _():
        relay_bottom.wait_recv()

    half_one(0)
    half_two(0)
    per_chunk = chunk // BX
    for i in range(CHUNKS):
        retreat(0, 1 + i * per_chunk, 1 + (i + 1) * per_chunk)

        @pl.when(has_prev)
        def _(i=i):
            back_copy(i).start()

    out0 = pltpu.make_async_copy(adj.at[0], adjoint_out.at[0], out_sem.at[2])
    out0.start()

    for i in range(CHUNKS):
        @pl.when(has_next)
        def _(i=i):
            back_copy(i).wait_recv()

        def body(b, carry):
            adj[1, at(b), :] = w[1, at(b + 1), :] - back[at(b), :]
            return carry

        lax.fori_loop(i * per_chunk, (i + 1) * per_chunk, body, 0)
    out1 = pltpu.make_async_copy(adj.at[1], adjoint_out.at[1], out_sem.at[3])
    out1.start()

    for side, there in sent_to:
        @pl.when(there)
        def _(side=side):
            for copy in to_side[side]:
                copy.wait_send()

    @pl.when(has_next)
    def _():
        forward.wait_send()

    @pl.when(has_next & has_lo)
    def _():
        relay_top.wait_send()

    @pl.when(has_next & has_hi)
    def _():
        relay_bottom.wait_send()

    @pl.when(has_prev)
    def _():
        for i in range(CHUNKS):
            back_copy(i).wait_send()

    for copy in misfit_copies:
        copy.wait()
    out0.wait()
    out1.wait()


def on_device(increments, precision, courant_rows, courant_cols, wind_codes):
    steps, rows, cols = increments.shape
    ext = rows + 2 * BX
    f32 = jnp.float32
    anywhere = pl.BlockSpec(memory_space=pl.ANY)
    out = jax.ShapeDtypeStruct(increments.shape, f32)
    field = pltpu.VMEM((2, ext, cols), f32)
    dma = pltpu.SemaphoreType.DMA
    return pl.pallas_call(
        kernel,
        name="window",
        out_shape=(out, out),
        in_specs=[anywhere] * 5,
        out_specs=(anywhere, anywhere),
        scratch_shapes=[
            pltpu.VMEM((3, ext, cols), f32),
            field,
            field,
            pltpu.VMEM((3,) + wind_codes.shape, jnp.int32),
            pltpu.VMEM((2, 3 * (rows // BX), cols), jnp.int32),
            field,
            field,
            field,
            field,
            field,
            field,
            pltpu.VMEM((2, rows, cols), f32),
            pltpu.VMEM((rows, cols), f32),
            pltpu.VMEM((2, rows, cols), f32),
            dma((5,)),
            dma((4,)),
            dma((2, 5)),
            dma((2, 5)),
            dma((3,)),
            dma((3,)),
            dma((CHUNKS,)),
            dma((CHUNKS,)),
        ],
        compiler_params=pltpu.CompilerParams(
            collective_id=0, has_side_effects=True, vmem_limit_bytes=40 << 20
        ),
    )(increments, precision, courant_rows, courant_cols, wind_codes)


def solution(mesh):
    in_specs = (
        P("tm", "space", None),
        P("tm", "space", None),
        P("space", None),
        P("space", None),
        P("tm", "space", None),
    )
    out_specs = (P("tm", "space", None), P("tm", "space", None))
    return jax.shard_map(
        on_device, mesh=mesh, in_specs=in_specs, out_specs=out_specs, check_vma=False
    )
```

time: 73.2 us -> 40.7 us (0.56); the launches traced: 71.9 us -> 40.4 us
  Pallas kernels: 0 us -> 32.6 us
  waiting for transfers between devices: 27.5 us -> 0 us
  starting transfers between devices: 26 us -> 0 us
  other arithmetic: 9.29 us -> 0 us
  local copies, waits for them, and re-layouts: 8.12 us -> 7.16 us
    pallas_call x0 -> x1, Pallas kernels: none -> 32.6 us  [on_device(): pl.pallas_call(kernel, name='window', out_shape=(out, out), in_specs=[any...]
    ppermute x10 -> x0, waiting for transfers between devices: 27.5 us -> none  [the longest x4 17.7 us: passed_along(): lax.ppermute(value, axis, [(source, source + steps) for source in range(f...]
    ppermute x10 -> x0, starting transfers between devices: 26 us -> none  [the longest x4 12.4 us: passed_along(): lax.ppermute(value, axis, [(source, source + steps) for source in range(f...]
    unnamed x12, local copies, waits for them, and re-layouts: 0.89 us -> 7.16 us
    select_n x4 -> x0, other arithmetic: 3.97 us -> none  [the longest x2 1.45 us: smooth(): field = jnp.where(inside[None, :, None], updated, 0.0)]
    slice x14 -> x0, local copies, waits for them, and re-layouts: 2.38 us -> none  [the longest x4 1.32 us: smooth(): jnp.roll(middle, -1, axis=2)]
    sub x3 -> x0, other arithmetic: 2.11 us -> none  [the longest x1 1.95 us: on_device(): misfit = increments - moved]
    squeeze x1 -> x0, local copies, waits for them, and re-layouts: 2.07 us -> none  [on_device(): incoming = passed_along(increments[1], 'tm', 1)]
  transfers between devices with their start and end apart: 10 -> 0, of which waited for: 6 -> 0; matrix products, arithmetic and copies ran while one was open for 5% -> 0% of each run, Pallas kernels for 0% -> 0%
where the time goes in v1:
time: 40.7 us; the launch traced here: 40.4 us
  Pallas kernels  32.6 us (80%)
  local copies, waits for them, and re-layouts  7.16 us (18%)
  between operations  0.65 us (2%)
    pallas_call x1, Pallas kernels, on_device(): pl.pallas_call(kernel, name='window', out_shape=(out, out), in_specs=[any...  32.6 us
    unnamed x12, local copies, waits for them, and re-layouts  7.16 us

profile of v1, /device:TPU:1, one launch (start us, length us, event | category | flops | bytes accessed | tf_op | source)
XLA Modules:
  0.0 40.4 jit_solution(10892971938223069260)
XLA Ops:
  0.6 0.0 copy-start
  0.6 1.2 %copy-done = f32[2,64,2048]{2,1,0:T(8,128)S(1)} copy-done((f32[2,64,2048]{2,1,0:T(8,128)S(1)}, f32[2,64,2048]{2,1,0:T(8,128)}, u32[]{:S(2)}) %copy-start) | copy-done | bytes 1048600
  1.9 0.0 copy-start.1
  1.9 1.2 %copy-done.1 = f32[2,64,2048]{2,1,0:T(8,128)S(1)} copy-done((f32[2,64,2048]{2,1,0:T(8,128)S(1)}, f32[2,64,2048]{2,1,0:T(8,128)}, u32[]{:S(2)}) %copy-start.1) | copy-done | bytes 1048600
  3.1 0.0 copy-start.2
  3.1 1.0 %copy-done.2 = f32[64,2048]{1,0:T(8,128)S(1)} copy-done((f32[64,2048]{1,0:T(8,128)S(1)}, f32[64,2048]{1,0:T(8,128)}, u32[]{:S(2)}) %copy-start.2) | copy-done | bytes 524312
  4.1 0.0 copy-start.3
  4.1 1.0 %copy-done.3 = f32[64,2048]{1,0:T(8,128)S(1)} copy-done((f32[64,2048]{1,0:T(8,128)S(1)}, f32[64,2048]{1,0:T(8,128)}, u32[]{:S(2)}) %copy-start.3) | copy-done | bytes 524312
  5.2 0.0 copy-start.4
  5.2 0.7 %copy-done.4 = s32[2,8,16]{2,1,0:T(8,128)S(1)} copy-done((s32[2,8,16]{2,1,0:T(8,128)S(1)}, s32[2,8,16]{2,1,0:T(8,128)}, u32[]{:S(2)}) %copy-start.4) | copy-done | bytes 1048
  5.9 32.6 %window.1 = (f32[2,64,2048]{2,1,0:T(8,128)S(1)}, f32[2,64,2048]{2,1,0:T(8,128)S(1)}) custom-call(f32[2,64,2048]{2,1,0:T(8,128)S(1)} %copy-done, f32[2,64,2048]{2,1,0:T(8,128)S(1)} %copy-done.1, f32[64,2048]{1,0:T(8,128)S(1)} %copy-done.2, f32[64,2048]{1,0:T(8,128)S(1)} %copy-done.3, s32[2,8,16]{2,1,0:T(8,128)S(1)} %copy-done.4), custom_call_target="tpu_custom_call" | custom-call | tf_op jit(solution)/shard_map/window/pallas_call | solution.py:341
  38.5 1.0 %copy.9 = f32[2,64,2048]{2,1,0:T(8,128)} copy(f32[2,64,2048]{2,1,0:T(8,128)S(1)} %get-tuple-element.4) | data formatting | bytes 2097152
  39.4 1.0 %copy.10 = f32[2,64,2048]{2,1,0:T(8,128)} copy(f32[2,64,2048]{2,1,0:T(8,128)S(1)} %get-tuple-element.5) | data formatting | bytes 2097152
Async XLA Ops:
  0.6 1.2 %copy-start = (f32[2,64,2048]{2,1,0:T(8,128)S(1)}, f32[2,64,2048]{2,1,0:T(8,128)}, u32[]{:S(2)}) copy-start(f32[2,64,2048]{2,1,0:T(8,128)} %inc.1) | copy-start | bytes 3145732
  1.9 1.2 %copy-start.1 = (f32[2,64,2048]{2,1,0:T(8,128)S(1)}, f32[2,64,2048]{2,1,0:T(8,128)}, u32[]{:S(2)}) copy-start(f32[2,64,2048]{2,1,0:T(8,128)} %prec.1) | copy-start | bytes 3145732
  3.1 1.0 %copy-start.2 = (f32[64,2048]{1,0:T(8,128)S(1)}, f32[64,2048]{1,0:T(8,128)}, u32[]{:S(2)}) copy-start(f32[64,2048]{1,0:T(8,128)} %crow.1) | copy-start | bytes 1572868
  4.1 1.0 %copy-start.3 = (f32[64,2048]{1,0:T(8,128)S(1)}, f32[64,2048]{1,0:T(8,128)}, u32[]{:S(2)}) copy-start(f32[64,2048]{1,0:T(8,128)} %ccol.1) | copy-start | bytes 1572868
  5.2 0.7 %copy-start.4 = (s32[2,8,16]{2,1,0:T(8,128)S(1)}, s32[2,8,16]{2,1,0:T(8,128)}, u32[]{:S(2)}) copy-start(s32[2,8,16]{2,1,0:T(8,128)} %codes.1) | copy-start | bytes 3076

commit v2 on v1

--- a/solution.py
+++ b/solution.py
@@ -10,14 +10,18 @@
 BX = 8
 BY = 128
 SWEEPS = 2
-CHUNKS = 4
 MESH = pl.DeviceIdType.MESH
+
+
+def chunks_of(blocks):
+    middle = [(b, min(2, blocks - b)) for b in range(2, blocks, 2)]
+    return middle + [(1, 1), (blocks, 1)]
 
 
 def kernel(
     inc, prec, crow, ccol, codes,
     misfit_out, adjoint_out,
-    incx, precx, cx, codex, cexp, ms, fa, fb, w, dn, up_, img, back, adj,
+    incx, precx, cx, codex, cexp, ms, f1, f2, f3, w, dn, up_, img, back, adj,
     local_sem, out_sem, zsend, zrecv, tsend, trecv, bsend, brecv,
 ):
     rows, cols = crow.shape
@@ -34,7 +38,7 @@
     bottom = pl.ds(BX + rows, BX)
     first = pl.ds(0, BX)
     last = pl.ds(rows - BX, BX)
-    chunk = rows // CHUNKS
+    parts = chunks_of(blocks)
 
     neighbours = (
         (has_lo, {"space": s - 1}),
@@ -88,8 +92,8 @@
     relay_bottom = remote(incx.at[2, bottom], incx.at[0, bottom], tsend.at[2], trecv.at[2], {"tm": t + 1})
 
     def back_copy(i):
-        part = pl.ds(i * chunk, chunk)
-        return remote(img.at[0, part], back.at[part], bsend.at[i], brecv.at[i], {"tm": t - 1})
+        part = pl.ds((parts[i][0] - 1) * BX, parts[i][1] * BX)
+        return remote(img.at[part], back.at[part], bsend.at[i], brecv.at[i], {"tm": t - 1})
 
     @pl.when(has_next)
     def _():
@@ -135,22 +139,7 @@
             def _(side=side):
                 to_side[side][i].wait_recv()
 
-    loads[0].wait()
-    arrived(0)
-
-    @pl.when(has_next & has_lo)
-    def _():
-        relay_top.start()
-
-    @pl.when(has_next & has_hi)
-    def _():
-        relay_bottom.start()
-
-    for i in (1, 2, 3):
-        loads[i].wait()
-        arrived(i)
-
-    for part in range(3):
+    def expand(part):
         for k in range(2):
             value = codex[part, k]
             for j in range(cols // BY):
@@ -164,140 +153,158 @@
     def at(b):
         return pl.ds(pl.multiple_of(b * BX, BX), BX)
 
-    def above(ref, k, b, cur):
-        prev = ref[k, at(jnp.maximum(b - 1, 0)), :]
-        return pltpu.roll(jnp.where(is_last, prev, cur), 1, 0)
-
-    def below(ref, k, b, cur):
-        after = ref[k, at(jnp.minimum(b + 1, blocks + 1)), :]
-        return pltpu.roll(jnp.where(is_first, after, cur), BX - 1, 0)
-
     def left(cur):
         return pltpu.roll(cur, 1, 1)
 
     def right(cur):
         return pltpu.roll(cur, cols - 1, 1)
 
-    def inside(b, value):
-        keep = ((b > 0) | has_lo) & ((b < blocks + 1) | has_hi)
-        return jnp.where(keep, value, 0.0)
-
     def code_of(k, b):
         return jnp.broadcast_to(cexp[k, pl.ds(b + blocks - 1, 1), :], (BX, cols))
 
-    def star(ref, k, b):
-        cur = ref[k, at(b), :]
-        return cur + above(ref, k, b, cur) + below(ref, k, b, cur) + (left(cur) + right(cur))
-
-    def misfits(k):
-        def body(b, carry):
+    def stages(k, edges):
+        low, high = (0, blocks + 1) if edges else (1, blocks)
+
+        def each(body):
+            def step(i, carry):
+                body(i + jnp.where(i >= 2, blocks - 2, 0) if edges else i + 1)
+                return carry
+
+            trips = 4 if edges else blocks
+            lax.fori_loop(0, trips, step, 0, unroll=trips)
+
+        def above(ref, b, cur):
+            prev = ref[k, at(jnp.maximum(b - 1, low)), :]
+            return pltpu.roll(jnp.where(is_last, prev, cur), 1, 0)
+
+        def below(ref, b, cur):
+            after = ref[k, at(jnp.minimum(b + 1, high)), :]
+            return pltpu.roll(jnp.where(is_first, after, cur), BX - 1, 0)
+
+        def inside(b, value):
+            if not edges:
+                return value
+            keep = ((b > 0) | has_lo) & ((b < blocks + 1) | has_hi)
+            return jnp.where(keep, value, 0.0)
+
+        def star(ref, b):
+            cur = ref[k, at(b), :]
+            return cur + above(ref, b, cur) + below(ref, b, cur) + (left(cur) + right(cur))
+
+        def misfit(b):
             cur = incx[k, at(b), :]
             code = code_of(k, b)
-            from_rows = jnp.where(code % 2 == 0, above(incx, k, b, cur), below(incx, k, b, cur))
+            from_rows = jnp.where((code & 1) == 0, above(incx, b, cur), below(incx, b, cur))
             from_cols = jnp.where(code < 2, left(cur), right(cur))
             moved = cur + cx[0, at(b), :] * (from_rows - cur) + cx[1, at(b), :] * (from_cols - cur)
             ms[k, at(b), :] = inside(b, incx[k + 1, at(b), :] - moved)
-            return carry
-
-        lax.fori_loop(0, blocks + 2, body, 0)
-
-    def sweep(src, dst, k, scale=None):
-        def body(b, carry):
-            value = star(src, k, b)
-            if scale is not None:
-                value = scale[k, at(b), :] * value
-            dst[k, at(b), :] = inside(b, value)
-            return carry
-
-        lax.fori_loop(0, blocks + 2, body, 0)
-
-    def weigh(k):
-        def body(b, carry):
-            value = inside(b, star(fa, k, b) * (0.2 ** (2 * SWEEPS)))
-            code = code_of(k, b)
+
+        def first_sweep(b):
+            f1[k, at(b), :] = inside(b, star(ms, b))
+
+        def second_sweep(b):
+            f2[k, at(b), :] = inside(b, precx[k, at(b), :] * star(f1, b))
+
+        def third_sweep(b):
+            f3[k, at(b), :] = inside(b, star(f2, b))
+
+        def weigh(b):
+            value = inside(b, star(f3, b) * (0.2 ** (2 * SWEEPS)))
+            lower = (code_of(k, b) & 1) == 0
             along = cx[0, at(b), :] * value
             w[k, at(b), :] = value
-            dn[k, at(b), :] = jnp.where(code % 2 == 0, along, 0.0)
-            up_[k, at(b), :] = jnp.where(code % 2 == 0, 0.0, along)
+            dn[k, at(b), :] = jnp.where(lower, along, 0.0)
+            up_[k, at(b), :] = jnp.where(lower, 0.0, along)
+
+        for body in (misfit, first_sweep, second_sweep, third_sweep, weigh):
+            each(body)
+
+    def retreat(k, start, size):
+        def body(i, carry):
+            b = i + start
+            value = w[k, at(b), :]
+            d, u = dn[k, at(b), :], up_[k, at(b), :]
+            after, prev = dn[k, at(b + 1), :], up_[k, at(b - 1), :]
+            along = cx[1, at(b), :] * value
+            plus = jnp.where(code_of(k, b) < 2, along, 0.0)
+            image = (
+                value - (d + u) - along
+                + pltpu.roll(jnp.where(is_first, after, d), BX - 1, 0)
+                + pltpu.roll(jnp.where(is_last, prev, u), 1, 0)
+                + right(plus) + left(along - plus)
+            )
+            if k == 0:
+                img[at(b - 1), :] = image
+            else:
+                adj[0, at(b - 1), :] = w[0, at(b), :] - image
             return carry
 
-        lax.fori_loop(0, blocks + 2, body, 0)
-
-    def retreat(k, start, stop):
-        def body(b, carry):
-            value = w[k, at(b), :]
-            code = code_of(k, b)
-            d, u = dn[k, at(b), :], up_[k, at(b), :]
-            cols_part = cx[1, at(b), :] * value
-            plus = jnp.where(code < 2, cols_part, 0.0)
-            minus = cols_part - plus
-            image = (
-                value - (d + u) - cols_part
-                + below(dn, k, b, d) + above(up_, k, b, u)
-                + right(plus) + left(minus)
-            )
-            img[k, at(b - 1), :] = image
-            if k == 0:
-                adj[0, at(b - 1), :] = value - img[1, at(b - 1), :]
-            return carry
-
-        lax.fori_loop(start, stop, body, 0)
-
+        lax.fori_loop(0, size, body, 0, unroll=size)
+
+    def send_back(i):
+        retreat(0, *parts[i])
+
+        @pl.when(has_prev)
+        def _():
+            back_copy(i).start()
+
+    for i in (0, 1, 2, 3):
+        loads[i].wait()
+    expand(1)
+    loads[4].wait()
+    stages(1, False)
+
+    arrived(0)
+
+    @pl.when(has_next & has_lo)
+    def _():
+        relay_top.start()
+
+    @pl.when(has_next & has_hi)
+    def _():
+        relay_bottom.start()
+
+    @pl.when(has_prev)
+    def _():
+        forward.wait_recv()
+
+    stages(0, False)
+    for i in range(len(parts) - 2):
+        send_back(i)
+
+    for i in (1, 2, 3, 4):
+        arrived(i)
+    expand(0)
+    expand(2)
+
+    @pl.when(has_prev & has_lo)
+    def _():
+        relay_top.wait_recv()
+
+    @pl.when(has_prev & has_hi)
+    def _():
+        relay_bottom.wait_recv()
+
+    stages(0, True)
+    for i in (len(parts) - 2, len(parts) - 1):
+        send_back(i)
+    stages(1, True)
     misfit_copies = [
         pltpu.make_async_copy(ms.at[k, own], misfit_out.at[k], out_sem.at[k]) for k in range(2)
     ]
-
-    def half_one(k):
-        misfits(k)
-        misfit_copies[k].start()
-        sweep(ms, fa, k)
-
-    def half_two(k):
-        sweep(fa, fb, k, precx)
-        sweep(fb, fa, k)
-        weigh(k)
-
-    half_one(1)
-    loads[4].wait()
-    arrived(4)
-    half_two(1)
-    retreat(1, 1, blocks + 1)
-
-    @pl.when(has_prev)
-    def _():
-        forward.wait_recv()
-
-    @pl.when(has_prev & has_lo)
-    def _():
-        relay_top.wait_recv()
-
-    @pl.when(has_prev & has_hi)
-    def _():
-        relay_bottom.wait_recv()
-
-    half_one(0)
-    half_two(0)
-    per_chunk = chunk // BX
-    for i in range(CHUNKS):
-        retreat(0, 1 + i * per_chunk, 1 + (i + 1) * per_chunk)
-
-        @pl.when(has_prev)
-        def _(i=i):
-            back_copy(i).start()
-
+    for copy in misfit_copies:
+        copy.start()
+    retreat(1, 1, blocks)
     out0 = pltpu.make_async_copy(adj.at[0], adjoint_out.at[0], out_sem.at[2])
     out0.start()
 
-    for i in range(CHUNKS):
+    for i, (start, size) in enumerate(parts):
         @pl.when(has_next)
         def _(i=i):
             back_copy(i).wait_recv()
 
-        def body(b, carry):
-            adj[1, at(b), :] = w[1, at(b + 1), :] - back[at(b), :]
-            return carry
-
-        lax.fori_loop(i * per_chunk, (i + 1) * per_chunk, body, 0)
+        for b in range(start, start + size):
+            adj[1, at(b - 1), :] = w[1, at(b), :] - back[at(b - 1), :]
     out1 = pltpu.make_async_copy(adj.at[1], adjoint_out.at[1], out_sem.at[3])
     out1.start()
 
@@ -321,7 +328,7 @@
 
     @pl.when(has_prev)
     def _():
-        for i in range(CHUNKS):
+        for i in range(len(parts)):
             back_copy(i).wait_send()
 
     for copy in misfit_copies:
@@ -335,6 +342,7 @@
     ext = rows + 2 * BX
     f32 = jnp.float32
     anywhere = pl.BlockSpec(memory_space=pl.ANY)
+    in_hbm = pl.BlockSpec(memory_space=pltpu.MemorySpace.HBM)
     out = jax.ShapeDtypeStruct(increments.shape, f32)
     field = pltpu.VMEM((2, ext, cols), f32)
     dma = pltpu.SemaphoreType.DMA
@@ -342,7 +350,7 @@
         kernel,
         name="window",
         out_shape=(out, out),
-        in_specs=[anywhere] * 5,
+        in_specs=[in_hbm] * 5,
         out_specs=(anywhere, anywhere),
         scratch_shapes=[
             pltpu.VMEM((3, ext, cols), f32),
@@ -356,7 +364,8 @@
             field,
             field,
             field,
-            pltpu.VMEM((2, rows, cols), f32),
+            field,
+            pltpu.VMEM((rows, cols), f32),
             pltpu.VMEM((rows, cols), f32),
             pltpu.VMEM((2, rows, cols), f32),
             dma((5,)),
@@ -365,11 +374,11 @@
             dma((2, 5)),
             dma((3,)),
             dma((3,)),
-            dma((CHUNKS,)),
-            dma((CHUNKS,)),
+            dma((len(chunks_of(rows // BX)),)),
+            dma((len(chunks_of(rows // BX)),)),
         ],
         compiler_params=pltpu.CompilerParams(
-            collective_id=0, has_side_effects=True, vmem_limit_bytes=40 << 20
+            collective_id=0, has_side_effects=True, vmem_limit_bytes=60 << 20
         ),
     )(increments, precision, courant_rows, courant_cols, wind_codes)
 

time: 40.7 us -> 25.3 us (0.62)
  Pallas kernels: 32.6 us -> 21.1 us
  local copies, waits for them, and re-layouts: 7.16 us -> 3.36 us
    pallas_call x1, Pallas kernels: 32.6 us -> 21.1 us  [on_device(): pl.pallas_call(kernel, name='window', out_shape=(out, out), in_specs=[in_...]
    unnamed x12 -> x4, local copies, waits for them, and re-layouts: 7.16 us -> 3.36 us
where the time goes in v2:
time: 25.3 us; the launch traced here: 25.1 us
  Pallas kernels  21.1 us (83%)
  local copies, waits for them, and re-layouts  3.36 us (13%)
  between operations  0.65 us (3%)
    pallas_call x1, Pallas kernels, on_device(): pl.pallas_call(kernel, name='window', out_shape=(out, out), in_specs=[in_...  21.1 us
    unnamed x4, local copies, waits for them, and re-layouts  3.36 us

profile of v2, /device:TPU:1, one launch (start us, length us, event | category | flops | bytes accessed | tf_op | source)
XLA Modules:
  0.0 25.1 jit_solution(8010071589955281937)
XLA Ops:
  0.6 21.1 %window.1 = (f32[2,64,2048]{2,1,0:T(8,128)}, f32[2,64,2048]{2,1,0:T(8,128)}) custom-call(f32[2,64,2048]{2,1,0:T(8,128)} %inc.1, f32[2,64,2048]{2,1,0:T(8,128)} %prec.1, f32[64,2048]{1,0:T(8,128)} %crow.1, f32[64,2048]{1,0:T(8,128)} %ccol.1, s32[2,8,16]{2,1,0:T(8,128)} %codes.1), custom_call_target="tpu_custom_call" | custom-call | tf_op jit(solution)/shard_map/window/pallas_call | solution.py:349
  21.7 0.0 copy-start
  21.7 2.4 %copy.9 = f32[2,64,2048]{2,1,0:T(8,128)} copy(f32[2,64,2048]{2,1,0:T(8,128)} %get-tuple-element.4) | data formatting | bytes 2097152
  24.1 0.0 copy-done
  24.1 1.0 %copy.10 = f32[2,64,2048]{2,1,0:T(8,128)} copy(f32[2,64,2048]{2,1,0:T(8,128)S(1)} %copy-done) | data formatting | bytes 2097152
Async XLA Ops:
  21.7 2.4 %copy-start = (f32[2,64,2048]{2,1,0:T(8,128)S(1)}, f32[2,64,2048]{2,1,0:T(8,128)}, u32[]{:S(2)}) copy-start(f32[2,64,2048]{2,1,0:T(8,128)} %get-tuple-element.5) | copy-start | bytes 3145732

commit v3 on v2

--- a/solution.py
+++ b/solution.py
@@ -20,8 +20,8 @@
 
 def kernel(
     inc, prec, crow, ccol, codes,
-    misfit_out, adjoint_out,
-    incx, precx, cx, codex, cexp, ms, f1, f2, f3, w, dn, up_, img, back, adj,
+    misfit_out, adj,
+    incx, precx, cx, codex, cexp, ms, f1, f2, f3, w, dn, up_, img, back,
     local_sem, out_sem, zsend, zrecv, tsend, trecv, bsend, brecv,
 ):
     rows, cols = crow.shape
@@ -295,8 +295,6 @@
     for copy in misfit_copies:
         copy.start()
     retreat(1, 1, blocks)
-    out0 = pltpu.make_async_copy(adj.at[0], adjoint_out.at[0], out_sem.at[2])
-    out0.start()
 
     for i, (start, size) in enumerate(parts):
         @pl.when(has_next)
@@ -305,8 +303,6 @@
 
         for b in range(start, start + size):
             adj[1, at(b - 1), :] = w[1, at(b), :] - back[at(b - 1), :]
-    out1 = pltpu.make_async_copy(adj.at[1], adjoint_out.at[1], out_sem.at[3])
-    out1.start()
 
     for side, there in sent_to:
         @pl.when(there)
@@ -333,15 +329,13 @@
 
     for copy in misfit_copies:
         copy.wait()
-    out0.wait()
-    out1.wait()
 
 
 def on_device(increments, precision, courant_rows, courant_cols, wind_codes):
     steps, rows, cols = increments.shape
     ext = rows + 2 * BX
     f32 = jnp.float32
-    anywhere = pl.BlockSpec(memory_space=pl.ANY)
+    in_vmem = pl.BlockSpec(memory_space=pltpu.MemorySpace.VMEM)
     in_hbm = pl.BlockSpec(memory_space=pltpu.MemorySpace.HBM)
     out = jax.ShapeDtypeStruct(increments.shape, f32)
     field = pltpu.VMEM((2, ext, cols), f32)
@@ -351,7 +345,7 @@
         name="window",
         out_shape=(out, out),
         in_specs=[in_hbm] * 5,
-        out_specs=(anywhere, anywhere),
+        out_specs=(in_vmem, in_vmem),
         scratch_shapes=[
             pltpu.VMEM((3, ext, cols), f32),
             field,
@@ -367,9 +361,8 @@
             field,
             pltpu.VMEM((rows, cols), f32),
             pltpu.VMEM((rows, cols), f32),
-            pltpu.VMEM((2, rows, cols), f32),
             dma((5,)),
-            dma((4,)),
+            dma((2,)),
             dma((2, 5)),
             dma((2, 5)),
             dma((3,)),
@@ -378,9 +371,9 @@
             dma((len(chunks_of(rows // BX)),)),
         ],
         compiler_params=pltpu.CompilerParams(
-            collective_id=0, has_side_effects=True, vmem_limit_bytes=60 << 20
+            collective_id=0, has_side_effects=True, vmem_limit_bytes=24 << 20
         ),
-    )(increments, precision, courant_rows, courant_cols, wind_codes)
+    )(*(pltpu.with_memory_space_constraint(x, pltpu.MemorySpace.HBM) for x in (increments, precision, courant_rows, courant_cols, wind_codes)))
 
 
 def solution(mesh):

time: 25.3 us -> 23.1 us (0.913)
  local copies, waits for them, and re-layouts: 3.36 us -> 1.94 us
  Pallas kernels: 21.1 us -> 20.3 us
    unnamed x4 -> x2, local copies, waits for them, and re-layouts: 3.36 us -> 1.94 us
    pallas_call x1, Pallas kernels: 21.1 us -> 20.3 us  [on_device(): pl.pallas_call(kernel, name='window', out_shape=(out, out), in_specs=[in_...]
where the time goes in v3:
time: 23.1 us; the launch traced here: 22.9 us
  Pallas kernels  20.3 us (88%)
  local copies, waits for them, and re-layouts  1.94 us (8%)
  between operations  0.64 us (3%)
    pallas_call x1, Pallas kernels, on_device(): pl.pallas_call(kernel, name='window', out_shape=(out, out), in_specs=[in_...  20.3 us
    unnamed x2, local copies, waits for them, and re-layouts  1.94 us

profile of v3, /device:TPU:1, one launch (start us, length us, event | category | flops | bytes accessed | tf_op | source)
XLA Modules:
  0.0 22.9 jit_solution(420917040573040501)
XLA Ops:
  0.6 20.3 %window.1 = (f32[2,64,2048]{2,1,0:T(8,128)S(1)}, f32[2,64,2048]{2,1,0:T(8,128)S(1)}) custom-call(f32[2,64,2048]{2,1,0:T(8,128)} %inc.1, f32[2,64,2048]{2,1,0:T(8,128)} %prec.1, f32[64,2048]{1,0:T(8,128)} %crow.1, f32[64,2048]{1,0:T(8,128)} %ccol.1, s32[2,8,16]{2,1,0:T(8,128)} %codes.1), custom_call_target="tpu_custom_call" | custom-call | tf_op jit(solution)/shard_map/window/pallas_call | solution.py:343
  20.9 1.0 %copy.9 = f32[2,64,2048]{2,1,0:T(8,128)} copy(f32[2,64,2048]{2,1,0:T(8,128)S(1)} %get-tuple-element.4) | data formatting | bytes 2097152
  21.9 1.0 %copy.10 = f32[2,64,2048]{2,1,0:T(8,128)} copy(f32[2,64,2048]{2,1,0:T(8,128)S(1)} %get-tuple-element.5) | data formatting | bytes 2097152

commit v4 on v3

--- a/solution.py
+++ b/solution.py
@@ -14,7 +14,9 @@
 
 
 def chunks_of(blocks):
-    middle = [(b, min(2, blocks - b)) for b in range(2, blocks, 2)]
+    half = blocks // 2
+    middle = [(2, half - 2), (half, (blocks - half) // 2)]
+    middle.append((sum(middle[1]), blocks - sum(middle[1])))
     return middle + [(1, 1), (blocks, 1)]
 
 
@@ -87,7 +89,15 @@
             for i, (src, dst) in enumerate(pairs)
         ]
 
-    forward = remote(inc.at[1], incx.at[0, own], tsend.at[0], trecv.at[0], {"tm": t + 1})
+    half = blocks // 2
+    forward = [
+        remote(
+            inc.at[1, pl.ds(start * BX, size * BX)],
+            incx.at[0, pl.ds((start + 1) * BX, size * BX)],
+            tsend.at[sem], trecv.at[sem], {"tm": t + 1},
+        )
+        for sem, start, size in ((0, 0, half), (3, half, blocks - half))
+    ]
     relay_top = remote(incx.at[2, top], incx.at[0, top], tsend.at[1], trecv.at[1], {"tm": t + 1})
     relay_bottom = remote(incx.at[2, bottom], incx.at[0, bottom], tsend.at[2], trecv.at[2], {"tm": t + 1})
 
@@ -97,7 +107,8 @@
 
     @pl.when(has_next)
     def _():
-        forward.start()
+        for copy in forward:
+            copy.start()
 
     sent_to = ((0, has_lo), (1, has_hi))
     arrives = ((0, has_hi), (1, has_lo))
@@ -162,15 +173,14 @@
     def code_of(k, b):
         return jnp.broadcast_to(cexp[k, pl.ds(b + blocks - 1, 1), :], (BX, cols))
 
-    def stages(k, edges):
-        low, high = (0, blocks + 1) if edges else (1, blocks)
+    def stages(k, begin, end, low, high, edges=False):
 
         def each(body):
             def step(i, carry):
-                body(i + jnp.where(i >= 2, blocks - 2, 0) if edges else i + 1)
+                body(i + jnp.where(i >= 2, blocks - 2, 0) if edges else i + begin)
                 return carry
 
-            trips = 4 if edges else blocks
+            trips = 4 if edges else end - begin + 1
             lax.fori_loop(0, trips, step, 0, unroll=trips)
 
         def above(ref, b, cur):
@@ -252,7 +262,7 @@
         loads[i].wait()
     expand(1)
     loads[4].wait()
-    stages(1, False)
+    stages(1, 1, blocks, 1, blocks)
 
     arrived(0)
 
@@ -266,10 +276,17 @@
 
     @pl.when(has_prev)
     def _():
-        forward.wait_recv()
-
-    stages(0, False)
-    for i in range(len(parts) - 2):
+        forward[0].wait_recv()
+
+    stages(0, 1, half, 1, half)
+    send_back(0)
+
+    @pl.when(has_prev)
+    def _():
+        forward[1].wait_recv()
+
+    stages(0, half, blocks, half - 1, blocks)
+    for i in range(1, len(parts) - 2):
         send_back(i)
 
     for i in (1, 2, 3, 4):
@@ -285,10 +302,10 @@
     def _():
         relay_bottom.wait_recv()
 
-    stages(0, True)
+    stages(0, 0, blocks + 1, 0, blocks + 1, edges=True)
     for i in (len(parts) - 2, len(parts) - 1):
         send_back(i)
-    stages(1, True)
+    stages(1, 0, blocks + 1, 0, blocks + 1, edges=True)
     misfit_copies = [
         pltpu.make_async_copy(ms.at[k, own], misfit_out.at[k], out_sem.at[k]) for k in range(2)
     ]
@@ -312,7 +329,8 @@
 
     @pl.when(has_next)
     def _():
-        forward.wait_send()
+        for copy in forward:
+            copy.wait_send()
 
     @pl.when(has_next & has_lo)
     def _():
@@ -365,8 +383,8 @@
             dma((2,)),
             dma((2, 5)),
             dma((2, 5)),
-            dma((3,)),
-            dma((3,)),
+            dma((4,)),
+            dma((4,)),
             dma((len(chunks_of(rows // BX)),)),
             dma((len(chunks_of(rows // BX)),)),
         ],

time: 23.1 us -> 22.3 us (0.965)
  Pallas kernels: 20.3 us -> 19.6 us
    pallas_call x1, Pallas kernels: 20.3 us -> 19.6 us  [on_device(): pl.pallas_call(kernel, name='window', out_shape=(out, out), in_specs=[in_...]
where the time goes in v4:
time: 22.3 us; the launch traced here: 22.2 us
  Pallas kernels  19.6 us (88%)
  local copies, waits for them, and re-layouts  1.94 us (9%)
  between operations  0.64 us (3%)
    pallas_call x1, Pallas kernels, on_device(): pl.pallas_call(kernel, name='window', out_shape=(out, out), in_specs=[in_...  19.6 us
    unnamed x2, local copies, waits for them, and re-layouts  1.94 us

profile of v4, /device:TPU:1, one launch (start us, length us, event | category | flops | bytes accessed | tf_op | source)
XLA Modules:
  0.0 22.2 jit_solution(16442552131179294198)
XLA Ops:
  0.6 19.6 %window.1 = (f32[2,64,2048]{2,1,0:T(8,128)S(1)}, f32[2,64,2048]{2,1,0:T(8,128)S(1)}) custom-call(f32[2,64,2048]{2,1,0:T(8,128)} %inc.1, f32[2,64,2048]{2,1,0:T(8,128)} %prec.1, f32[64,2048]{1,0:T(8,128)} %crow.1, f32[64,2048]{1,0:T(8,128)} %ccol.1, s32[2,8,16]{2,1,0:T(8,128)} %codes.1), custom_call_target="tpu_custom_call" | custom-call | tf_op jit(solution)/shard_map/window/pallas_call | solution.py:361
  20.2 1.0 %copy.9 = f32[2,64,2048]{2,1,0:T(8,128)} copy(f32[2,64,2048]{2,1,0:T(8,128)S(1)} %get-tuple-element.4) | data formatting | bytes 2097152
  21.2 1.0 %copy.10 = f32[2,64,2048]{2,1,0:T(8,128)} copy(f32[2,64,2048]{2,1,0:T(8,128)S(1)} %get-tuple-element.5) | data formatting | bytes 2097152

commit v5 on v4

--- a/solution.py
+++ b/solution.py
@@ -38,8 +38,7 @@
     own = pl.ds(BX, rows)
     top = pl.ds(0, BX)
     bottom = pl.ds(BX + rows, BX)
-    first = pl.ds(0, BX)
-    last = pl.ds(rows - BX, BX)
+    depths = (2 * SWEEPS + 2, 2 * SWEEPS + 1, SWEEPS + 1)
     parts = chunks_of(blocks)
 
     neighbours = (
@@ -73,16 +72,19 @@
             device_id=where, device_id_type=MESH,
         )
 
+    def halo_rows(side, n):
+        return pl.ds(BX + rows if side == 0 else BX - n, n)
+
     def z_copies(side):
-        edge = first if side == 0 else last
-        halo = bottom if side == 0 else top
         where = {"space": s - 1} if side == 0 else {"space": s + 1}
+        edge = [pl.ds(0 if side == 0 else rows - n, n) for n in depths]
+        halo = [halo_rows(side, n) for n in depths]
         pairs = [
-            (inc.at[:, edge], incx.at[pl.ds(1, 2), halo]),
-            (crow.at[edge], cx.at[0, halo]),
-            (ccol.at[edge], cx.at[1, halo]),
+            (inc.at[:, edge[0]], incx.at[pl.ds(1, 2), halo[0]]),
+            (crow.at[edge[1]], cx.at[0, halo[1]]),
+            (ccol.at[edge[1]], cx.at[1, halo[1]]),
             (codes, codex.at[2 if side == 0 else 0]),
-            (prec.at[:, edge], precx.at[:, halo]),
+            (prec.at[:, edge[2]], precx.at[:, halo[2]]),
         ]
         return [
             remote(src, dst, zsend.at[side, i], zrecv.at[side, i], where)
@@ -98,8 +100,10 @@
         )
         for sem, start, size in ((0, 0, half), (3, half, blocks - half))
     ]
-    relay_top = remote(incx.at[2, top], incx.at[0, top], tsend.at[1], trecv.at[1], {"tm": t + 1})
-    relay_bottom = remote(incx.at[2, bottom], incx.at[0, bottom], tsend.at[2], trecv.at[2], {"tm": t + 1})
+    relay_top = remote(
+        incx.at[2, halo_rows(1, depths[0])], incx.at[0, halo_rows(1, depths[0])], tsend.at[1], trecv.at[1], {"tm": t + 1})
+    relay_bottom = remote(
+        incx.at[2, halo_rows(0, depths[0])], incx.at[0, halo_rows(0, depths[0])], tsend.at[2], trecv.at[2], {"tm": t + 1})
 
     def back_copy(i):
         part = pl.ds((parts[i][0] - 1) * BX, parts[i][1] * BX)

time: 22.3 us -> 21.2 us (0.951)
  Pallas kernels: 19.6 us -> 18.4 us
    pallas_call x1, Pallas kernels: 19.6 us -> 18.4 us  [on_device(): pl.pallas_call(kernel, name='window', out_shape=(out, out), in_specs=[in_...]
where the time goes in v5:
time: 21.2 us; the launch traced here: 20.9 us
  Pallas kernels  18.4 us (87%)
  local copies, waits for them, and re-layouts  1.94 us (9%)
  between operations  0.64 us (3%)
    pallas_call x1, Pallas kernels, on_device(): pl.pallas_call(kernel, name='window', out_shape=(out, out), in_specs=[in_...  18.4 us
    unnamed x2, local copies, waits for them, and re-layouts  1.94 us

profile of v5, /device:TPU:1, one launch (start us, length us, event | category | flops | bytes accessed | tf_op | source)
XLA Modules:
  0.0 20.9 jit_solution(15566144850060614131)
XLA Ops:
  0.6 18.4 %window.1 = (f32[2,64,2048]{2,1,0:T(8,128)S(1)}, f32[2,64,2048]{2,1,0:T(8,128)S(1)}) custom-call(f32[2,64,2048]{2,1,0:T(8,128)} %inc.1, f32[2,64,2048]{2,1,0:T(8,128)} %prec.1, f32[64,2048]{1,0:T(8,128)} %crow.1, f32[64,2048]{1,0:T(8,128)} %ccol.1, s32[2,8,16]{2,1,0:T(8,128)} %codes.1), custom_call_target="tpu_custom_call" | custom-call | tf_op jit(solution)/shard_map/window/pallas_call | solution.py:365
  19.0 1.0 %copy.9 = f32[2,64,2048]{2,1,0:T(8,128)} copy(f32[2,64,2048]{2,1,0:T(8,128)S(1)} %get-tuple-element.4) | data formatting | bytes 2097152
  20.0 1.0 %copy.10 = f32[2,64,2048]{2,1,0:T(8,128)} copy(f32[2,64,2048]{2,1,0:T(8,128)S(1)} %get-tuple-element.5) | data formatting | bytes 2097152
